TPU v7x, 32 devices: a whole 2x2x4 slice. The times are simulated.
32 devices in a mesh: row: 8 (over z, y), col: 4 (over x, core).
Axes of the slice: x: 2, y: 2, z: 4, core: 2. Of those that a mesh axis runs over, the one named last changes fastest.
Arguments:
- trailing: bfloat16 [12288, 12288], P('row', 'col'), may hold values from -6 to 6
- rows_a: int32 [8, 12], replicated, may hold values from 0 to 11, as said below
- counts_a: int32 [8], replicated, may hold values from 1 to 12, as said below
- factor_a: bfloat16 [12288, 512], P('row'), may hold values from -0.0546875 to 0.0546875
- rows_b: int32 [8, 12], replicated, may hold values from 0 to 11, as said below
- counts_b: int32 [8], replicated, may hold values from 1 to 12, as said below
- factor_b: bfloat16 [12288, 512], P('row'), may hold values from -0.0546875 to 0.0546875
- factor_top: bfloat16 [512, 512], replicated, may hold values from -0.25 to 0.25
- base_a: float32 [512, 512], P('col'), may hold values from -3 to 3
- base_b: float32 [512, 512], P('col'), may hold values from -3 to 3
Outputs:
- column_a: bfloat16 [12288, 512], P('row')
- diag_a: float32 [512, 512], P('col')
- column_b: bfloat16 [12288, 512], P('row')
- top_b: bfloat16 [512, 512], P('col')
- diag_b: float32 [512, 512], P('col')
Inputs may be any that keep to these rules, and one draw needn't show every extreme that they name: `rows_a`: the first counts_a[r] entries of row r are distinct; the rest of the row is padding. `counts_a`: some owner uses all 12 slots in every draw. `rows_b`: the first counts_b[r] entries of row r are distinct and lie among the first counts_a[r] entries of row r of rows_a; the rest is padding. counts_b[r] <= counts_a[r]; some owner uses all 12 slots in every draw.
All inputs are finite; a program needn't handle non-finite values.
Results may differ from a plain program's by a relative error of at most 0.007.
Values may be sent and summed in bfloat16 or wider, within the bound.
A program may use at most 128 MiB of HBM per device.

v0:
```python
import jax
import jax.numpy as jnp
from jax import lax
from jax.sharding import PartitionSpec as P


def contract_rows(former, latter):
    return lax.dot_general(
        former, latter, (((0,), (0,)), ((), ())), preferred_element_type=jnp.float32
    )


def on_device(
    trailing, rows_a, counts_a, factor_a, rows_b, counts_b, factor_b, factor_top, base_a, base_b
):
    row_count = lax.axis_size("row")
    col_count = lax.axis_size("col")
    fanout = row_count // col_count
    row_index = lax.axis_index("row")
    col_index = lax.axis_index("col")
    slots = rows_a.shape[1]
    total_rows, width = factor_a.shape
    block = total_rows // slots
    row_blocks = trailing.shape[0] // block
    part_width = width // col_count
    width_start = col_index * part_width
    slot_ids = jnp.arange(slots, dtype=jnp.int32)

    def own(table):
        return lax.dynamic_index_in_dim(table, row_index, 0, keepdims=False)

    live_a = slot_ids < own(counts_a)
    live_b = slot_ids < own(counts_b)
    own_a, own_b = (own(rows_a), own(rows_b))
    blocks = jnp.arange(row_blocks, dtype=jnp.int32)
    gate_a = jnp.any((own_a[None, :] == blocks[:, None]) & live_a[None, :], axis=1)
    gate_b = jnp.any((own_b[None, :] == blocks[:, None]) & live_b[None, :], axis=1)
    pieces = jnp.stack([factor_a, factor_b]).reshape(2, row_count, total_rows // row_count, width)
    arrived = []
    for shift in range(row_count):
        piece = lax.dynamic_index_in_dim(pieces, (row_index + shift) % row_count, 1, keepdims=False)
        if shift:
            pairs = [
                (
                    owner * col_count + owner % col_count,
                    (owner + shift) % row_count * col_count + owner % col_count,
                )
                for owner in range(row_count)
            ]
            piece = lax.ppermute(piece, ("row", "col"), pairs)
        arrived.append(piece)
    arrived = jnp.stack(arrived)
    mine = jnp.stack(
        [
            lax.dynamic_index_in_dim(
                arrived, (row_index - col_index - part * col_count) % row_count, 0, keepdims=False
            )
            for part in range(fanout)
        ],
        axis=1,
    )
    held = lax.all_gather(mine, "row", axis=2, tiled=True)
    owners = col_index + jnp.arange(fanout, dtype=jnp.int32) * col_count

    def partial_product(node, rows, counts):
        own_rows = jnp.take(rows, owners, axis=0)
        live = slot_ids[None, :] < jnp.take(counts, owners, axis=0)[:, None]
        match = (own_rows[None, :, :] == blocks[:, None, None]) & live[None, :, :]
        filled = jnp.any(match, axis=2).reshape(-1)
        source = jnp.argmax(match, axis=2).astype(jnp.int32)
        source = (source + jnp.arange(fanout, dtype=jnp.int32) * slots).reshape(-1)
        picked = jnp.take(held[node].reshape(fanout * slots, block, width), source, axis=0)
        spread = jnp.where(filled[:, None, None], picked, 0).reshape(-1, width)
        return jnp.dot(trailing, spread, preferred_element_type=jnp.float32).astype(jnp.bfloat16)

    part = jnp.stack([partial_product(0, rows_a, counts_a), partial_product(1, rows_b, counts_b)])
    reduced = lax.psum_scatter(part, "col", scatter_dimension=2, tiled=True).astype(jnp.float32)

    def gated(value, gate):
        return jnp.where(gate[:, None, None], value.reshape(row_blocks, block, -1), 0).reshape(
            row_blocks * block, -1
        )

    def by_slot(value, own_rows, live):
        picked = jnp.take(value.reshape(row_blocks, block, -1), own_rows, axis=0)
        return jnp.where(live[:, None, None], picked, 0).reshape(total_rows, -1)

    col_a = gated(-reduced[0], gate_a).astype(jnp.bfloat16)
    whole_a = lax.all_gather(col_a, "col", axis=1, tiled=True)
    column_a = by_slot(whole_a, own_a, live_a)
    top_part = lax.dynamic_slice_in_dim(factor_top, width_start, part_width, 1)
    cross = jnp.dot(whole_a, top_part, preferred_element_type=jnp.float32)
    col_b = gated(-(reduced[1] + cross), gate_b).astype(jnp.bfloat16)
    column_b = by_slot(lax.all_gather(col_b, "col", axis=1, tiled=True), own_b, live_b)
    sums = lax.psum(
        (
            contract_rows(by_slot(col_a, own_a, live_a), factor_a),
            contract_rows(by_slot(col_a, own_b, live_b), factor_b),
            contract_rows(by_slot(col_b, own_b, live_b), factor_b),
        ),
        "row",
    )
    diag_a = base_a - sums[0]
    top_b = (
        -(
            sums[1]
            + jnp.dot(diag_a, factor_top.astype(jnp.float32), precision=lax.Precision.HIGHEST)
        )
    ).astype(jnp.bfloat16)
    top_whole = lax.all_gather(top_b, "col", axis=0, tiled=True)
    top_cols = lax.dynamic_slice_in_dim(top_whole, width_start, part_width, 1)
    diag_b = base_b - sums[2] - contract_rows(top_cols, factor_top)
    return (column_a, diag_a, column_b, top_b, diag_b)


def solution(mesh):
    in_specs = (
        P("row", "col"),
        P(),
        P(),
        P("row", None),
        P(),
        P(),
        P("row", None),
        P(),
        P("col", None),
        P("col", None),
    )
    out_specs = (P("row", None), P("col", None), P("row", None), P("col", None), P("col", None))
    return jax.shard_map(
        on_device, mesh=mesh, in_specs=in_specs, out_specs=out_specs, check_vma=False
    )
```

profile of v0, /device:TPU:0, one launch (start us, length us, event | category | flops | bytes accessed | tf_op | source)
XLA Modules:
  0.0 359.1 jit_solution(10162166294966140)
XLA Ops:
  7.3 2.9 fusion.22
  10.2 5.7 %collective-permute-start = (bf16[2,192,512]{2,1,0:T(8,128)(2,1)}, bf16[2,192,512]{2,1,0:T(8,128)(2,1)}, u32[]{:S(2)}, u32[]{:S(2)}) collective-permute-start(bf16[2,192,512]{2,1,0:T(8,128)(2,1)} %get-tuple-element.26), channel_id=1, source_target_pairs={{0,4},{5,9},{10,14},{15,19},{16,20},{21,25},{26,30},{31,3}} | collective-permute-start | bytes 1179656 | tf_op jit(solution)/shard_map/ppermute | solution.py:50
  15.9 2.1 collective-permute-start.1
  18.0 2.0 collective-permute-start.2
  20.0 4.5 %collective-permute-start.3 = (bf16[2,192,512]{2,1,0:T(8,128)(2,1)S(1)}, bf16[2,192,512]{2,1,0:T(8,128)(2,1)}, u32[]{:S(2)}, u32[]{:S(2)}) collective-permute-start(bf16[2,192,512]{2,1,0:T(8,128)(2,1)S(1)} %get-tuple-element.29), channel_id=1, source_target_pairs={{0,16},{5,21},{10,26},{15,31},{16,0},{21,5},{26,10},{31,15}} | collective-permute-start | bytes 1179656 | tf_op jit(solution)/shard_map/ppermute | solution.py:50
  24.5 2.1 collective-permute-start.4
  26.6 1.7 bitcast_dynamic-update-slice_fusion.7
  37.3 2.3 collective-permute-done.5
  39.6 4.2 %collective-permute-done.6 = bf16[2,192,512]{2,1,0:T(8,128)(2,1)S(1)} collective-permute-done((bf16[2,192,512]{2,1,0:T(8,128)(2,1)S(1)}, bf16[2,192,512]{2,1,0:T(8,128)(2,1)S(1)}, u32[]{:S(2)}, u32[]{:S(2)}) %collective-permute-start.6) | collective-permute-done | bytes 393248 | tf_op jit(solution)/shard_map/ppermute | solution.py:50
  50.7 95.2 %all-gather.4.cloned.1.call-done = bf16[2,2,1536,512]{3,2,0,1:T(8,128)(2,1)} async-done(((bf16[2,2,192,512]{3,2,0,1:T(8,128)(2,1)}), bf16[2,2,1536,512]{3,2,0,1:T(8,128)(2,1)}) %all-gather.4.cloned.1.call-update) | async-done | bytes 6291472 | tf_op jit(solution)/shard_map/all_gather | solution.py:62
  145.9 5.9 %fusion.37 = (bf16[1,2,1536,512]{3,2,0,1:T(8,128)(2,1)}, bf16[1,2,1536,512]{3,2,0,1:T(8,128)(2,1)}) fusion(bf16[2,2,1536,512]{3,2,0,1:T(8,128)(2,1)} %all-gather.4.cloned.1.call-done), kind=kLoop, calls=%fused_computation.126 | loop fusion | bytes 12582912 | tf_op jit(solution)/shard_map/slice | solution.py:72
  151.8 4.4 %gather_fusion.2 = bf16[24,128,512]{2,1,0:T(8,128)(2,1)} fusion(bf16[24,128,512]{2,1,0:T(8,128)(2,1)} %bitcast.98, s32[1024]{0:T(1024)S(1)} %pad_clamp_fusion.3), kind=kCustom, calls=%fused_computation.2.clone | custom fusion | bytes 6291552 | tf_op jit(solution)/shard_map/jit(_take)/gather | solution.py:72
  156.2 2.3 select_select_fusion.1
  158.5 9.0 %fusion = bf16[1,1536,512]{1,2,0:T(8,128)(2,1)} fusion(bf16[3072,512]{1,0:T(8,128)(2,1)S(1)} %bitcast.101, bf16[1536,3072]{1,0:T(8,128)(2,1)} %param.20), kind=kOutput, calls=%fused_computation.32 | convolution fusion | flops 4832624640 | bytes 14155776 | tf_op jit(solution)/shard_map/dot_general | solution.py:74
  167.5 4.4 %gather_fusion.5 = bf16[24,128,512]{2,1,0:T(8,128)(2,1)} fusion(bf16[24,128,512]{2,1,0:T(8,128)(2,1)} %bitcast.97, s32[1024]{0:T(1024)S(1)} %pad_clamp_fusion.2), kind=kCustom, calls=%fused_computation.7.clone | custom fusion | bytes 6291552 | tf_op jit(solution)/shard_map/jit(_take)/gather | solution.py:72
  171.9 2.3 select_select_fusion
  174.2 8.0 %fusion.1 = bf16[1,1536,512]{1,2,0:T(8,128)(2,1)S(1)} fusion(bf16[3072,512]{1,0:T(8,128)(2,1)S(1)} %bitcast.102, bf16[1536,3072]{1,0:T(8,128)(2,1)} %param.20), kind=kOutput, calls=%fused_computation.33 | convolution fusion | flops 4832624640 | bytes 14155776 | tf_op jit(solution)/shard_map/dot_general | solution.py:74
  182.2 1.9 pad_maximum_fusion
  186.2 34.1 %reduce-scatter.2.cloned.1.call-done = bf16[2,1536,128]{1,2,0:T(8,128)(2,1)} async-done(((bf16[2,1536,512]{1,2,0:T(8,128)(2,1)}), bf16[2,1536,128]{1,2,0:T(8,128)(2,1)}) %reduce-scatter.2.cloned.1.call-update) | async-done | bytes 786448 | tf_op jit(solution)/shard_map/reduce_scatter | solution.py:77
  227.7 2.5 fusion.38
  230.2 13.2 %all-gather.6.cloned.1.call-done = bf16[1536,512]{0,1:T(8,128)(2,1)} async-done(((bf16[1536,128]{0,1:T(8,128)(2,1)}), bf16[1536,512]{0,1:T(8,128)(2,1)}) %all-gather.6.cloned.1.call-update) | async-done | bytes 1572880 | tf_op jit(solution)/shard_map/all_gather | solution.py:89
  243.4 2.0 fusion.4
  251.1 2.6 copy.27
  253.7 2.1 gather_fusion.6
  257.2 69.1 %all-reduce.3.cloned.1.call-done = (f32[128,512]{1,0:T(8,128)}, f32[128,512]{1,0:T(8,128)}, f32[128,512]{1,0:T(8,128)}) async-done(((f32[128,512]{1,0:T(8,128)}, f32[128,512]{1,0:T(8,128)}, f32[128,512]{1,0:T(8,128)}), (f32[128,512]{1,0:T(8,128)}, f32[128,512]{1,0:T(8,128)}, f32[128,512]{1,0:T(8,128)})) %all-reduce.3.cloned.1.call-update) | async-done | bytes 786448 | tf_op jit(solution)/shard_map/psum | solution.py:95
  327.3 1.4 fusion.6
  328.7 7.1 %all_gather.15 = bf16[512,512]{1,0:T(8,128)(2,1)S(1)} all-gather(bf16[128,512]{1,0:T(8,128)(2,1)S(1)} %fusion.6), channel_id=1, replica_groups=mesh['row'=8,'col'=4] {'col'}, dimensions={0}, use_global_device_ids=true | all-gather | bytes 655360 | tf_op jit(solution)/shard_map/all_gather | solution.py:110
  335.9 1.9 convolution_subtract_fusion
  337.8 8.7 %all-gather.8.cloned.1.call-done = bf16[1536,512]{0,1:T(8,128)(2,1)} async-done(((bf16[1536,128]{0,1:T(8,128)(2,1)}), bf16[1536,512]{0,1:T(8,128)(2,1)}) %all-gather.8.cloned.1.call-update) | async-done | bytes 1572880 | tf_op jit(solution)/shard_map/all_gather | solution.py:94
  346.5 2.6 copy.30
  349.1 2.1 gather_fusion.8
  351.2 1.4 select_select_fusion.2
  (108 shorter events, 33.1 us)
Async XLA Ops:
  7.2 236.2 %copy-start = (bf16[512,512]{1,0:T(8,128)(2,1)S(1)}, bf16[512,512]{1,0:T(8,128)(2,1)}, u32[]{:S(2)}) copy-start(bf16[512,512]{1,0:T(8,128)(2,1)} %param.27) | copy-start | bytes 1572868
  7.2 19.4 %copy-start.3 = (bf16[1536,512]{1,0:T(8,128)(2,1)S(1)}, bf16[1536,512]{1,0:T(8,128)(2,1)}, u32[]{:S(2)}) copy-start(bf16[1536,512]{1,0:T(8,128)(2,1)} %param.26) | copy-start | bytes 4718596
  7.2 138.7 %all-gather.4.cloned.1.call-start = ((), (), s32[]{:S(2)}) async-start(), calls=%async_computation.1 | async-start | bytes 7077888 | tf_op jit(solution)/shard_map/all_gather | solution.py:62
  10.2 19.1 %collective-permute-start = (bf16[2,192,512]{2,1,0:T(8,128)(2,1)}, bf16[2,192,512]{2,1,0:T(8,128)(2,1)}, u32[]{:S(2)}, u32[]{:S(2)}) collective-permute-start(bf16[2,192,512]{2,1,0:T(8,128)(2,1)} %get-tuple-element.26), channel_id=1, source_target_pairs={{0,4},{5,9},{10,14},{15,19},{16,20},{21,25},{26,30},{31,3}} | collective-permute-start | bytes 1179656 | tf_op jit(solution)/shard_map/ppermute | solution.py:50
  15.9 15.8 %collective-permute-start.1 = (bf16[2,192,512]{2,1,0:T(8,128)(2,1)}, bf16[2,192,512]{2,1,0:T(8,128)(2,1)}, u32[]{:S(2)}, u32[]{:S(2)}) collective-permute-start(bf16[2,192,512]{2,1,0:T(8,128)(2,1)} %get-tuple-element.27), channel_id=1, source_target_pairs={{0,8},{5,13},{10,18},{15,23},{16,24},{21,29},{26,2},{31,7}} | collective-permute-start | bytes 1179656 | tf_op jit(solution)/shard_map/ppermute | solution.py:50
  18.0 16.1 %collective-permute-start.2 = (bf16[2,192,512]{2,1,0:T(8,128)(2,1)}, bf16[2,192,512]{2,1,0:T(8,128)(2,1)}, u32[]{:S(2)}, u32[]{:S(2)}) collective-permute-start(bf16[2,192,512]{2,1,0:T(8,128)(2,1)} %get-tuple-element.28), channel_id=1, source_target_pairs={{0,12},{5,17},{10,22},{15,27},{16,28},{21,1},{26,6},{31,11}} | collective-permute-start | bytes 1179656 | tf_op jit(solution)/shard_map/ppermute | solution.py:50
  20.0 15.1 %collective-permute-start.3 = (bf16[2,192,512]{2,1,0:T(8,128)(2,1)S(1)}, bf16[2,192,512]{2,1,0:T(8,128)(2,1)}, u32[]{:S(2)}, u32[]{:S(2)}) collective-permute-start(bf16[2,192,512]{2,1,0:T(8,128)(2,1)S(1)} %get-tuple-element.29), channel_id=1, source_target_pairs={{0,16},{5,21},{10,26},{15,31},{16,0},{21,5},{26,10},{31,15}} | collective-permute-start | bytes 1179656 | tf_op jit(solution)/shard_map/ppermute | solution.py:50
  24.5 11.7 %collective-permute-start.4 = (bf16[2,192,512]{2,1,0:T(8,128)(2,1)S(1)}, bf16[2,192,512]{2,1,0:T(8,128)(2,1)}, u32[]{:S(2)}, u32[]{:S(2)}) collective-permute-start(bf16[2,192,512]{2,1,0:T(8,128)(2,1)S(1)} %get-tuple-element.30), channel_id=1, source_target_pairs={{0,20},{5,25},{10,30},{15,3},{16,4},{21,9},{26,14},{31,19}} | collective-permute-start | bytes 1179656 | tf_op jit(solution)/shard_map/ppermute | solution.py:50
  28.2 2.5 copy-start.9
  29.4 10.2 %collective-permute-start.5 = (bf16[2,192,512]{2,1,0:T(8,128)(2,1)S(1)}, bf16[2,192,512]{2,1,0:T(8,128)(2,1)S(1)}, u32[]{:S(2)}, u32[]{:S(2)}) collective-permute-start(bf16[2,192,512]{2,1,0:T(8,128)(2,1)S(1)} %fusion.16), channel_id=1, source_target_pairs={{0,24},{5,29},{10,2},{15,7},{16,8},{21,13},{26,18},{31,23}} | collective-permute-start | bytes 1179656 | tf_op jit(solution)/shard_map/ppermute | solution.py:50
  31.7 12.0 %collective-permute-start.6 = (bf16[2,192,512]{2,1,0:T(8,128)(2,1)S(1)}, bf16[2,192,512]{2,1,0:T(8,128)(2,1)S(1)}, u32[]{:S(2)}, u32[]{:S(2)}) collective-permute-start(bf16[2,192,512]{2,1,0:T(8,128)(2,1)S(1)} %get-tuple-element.25), channel_id=1, source_target_pairs={{0,28},{5,1},{10,6},{15,11},{16,12},{21,17},{26,22},{31,27}} | collective-permute-start | bytes 1179656 | tf_op jit(solution)/shard_map/ppermute | solution.py:50
  36.2 8.7 %copy-start.12 = (s32[8,12]{1,0:T(8,128)S(1)}, s32[8,12]{1,0:T(8,128)}, u32[]{:S(2)}) copy-start(s32[8,12]{1,0:T(8,128)} %param.21) | copy-start | bytes 1156
  36.2 9.3 %copy-start.13 = (s32[8,12]{1,0:T(8,128)S(1)}, s32[8,12]{1,0:T(8,128)}, u32[]{:S(2)}) copy-start(s32[8,12]{1,0:T(8,128)} %param.24) | copy-start | bytes 1156
  36.2 9.8 %copy-start.1 = (s32[8]{0:T(128)S(1)}, s32[8]{0:T(128)}, u32[]{:S(2)}) copy-start(s32[8]{0:T(128)} %param.22) | copy-start | bytes 100
  37.2 9.4 %copy-start.2 = (s32[8]{0:T(128)S(1)}, s32[8]{0:T(128)}, u32[]{:S(2)}) copy-start(s32[8]{0:T(128)} %param.25) | copy-start | bytes 100
  44.8 175.5 %reduce-scatter.2.cloned.1.call-start = ((), (), s32[]{:S(2)}) async-start(), calls=%async_computation.2 | async-start | bytes 3932160 | tf_op jit(solution)/shard_map/reduce_scatter | solution.py:77
  174.2 8.0 %copy-start.6 = (bf16[1,1536,512]{1,2,0:T(8,128)(2,1)S(1)}, bf16[1,1536,512]{1,2,0:T(8,128)(2,1)}, u32[]{:S(2)}) copy-start(bf16[1,1536,512]{1,2,0:T(8,128)(2,1)} %fusion) | copy-start | bytes 4718596
  184.1 59.3 %all-gather.6.cloned.1.call-start = ((), (), s32[]{:S(2)}) async-start(), calls=%async_computation.3 | async-start | bytes 1966080 | tf_op jit(solution)/shard_map/all_gather | solution.py:89
  221.6 1.1 copy-start.4
  223.6 102.7 %all-reduce.3.cloned.1.call-start = ((), (), s32[]{:S(2)}) async-start(), calls=%async_computation.5 | async-start | bytes 1572864 | tf_op jit(solution)/shard_map/psum | solution.py:95
  245.5 5.0 %copy-start.5 = (bf16[1536,128]{0,1:T(8,128)(2,1)}, bf16[1536,128]{0,1:T(8,128)(2,1)S(1)}, u32[]{:S(2)}) copy-start(bf16[1536,128]{0,1:T(8,128)(2,1)S(1)} %fusion.4) | copy-start | bytes 1179652
  250.5 96.0 %all-gather.8.cloned.1.call-start = ((), (), s32[]{:S(2)}) async-start(), calls=%async_computation.4 | async-start | bytes 1966080 | tf_op jit(solution)/shard_map/all_gather | solution.py:94
  253.7 72.6 %copy-start.10 = (f32[128,512]{1,0:T(8,128)S(1)}, f32[128,512]{1,0:T(8,128)}, u32[]{:S(2)}) copy-start(f32[128,512]{1,0:T(8,128)} %param.28) | copy-start | bytes 786436
  255.8 80.1 %copy-start.11 = (f32[128,512]{1,0:T(8,128)S(1)}, f32[128,512]{1,0:T(8,128)}, u32[]{:S(2)}) copy-start(f32[128,512]{1,0:T(8,128)} %param.29) | copy-start | bytes 786436
  327.3 21.8 %copy-start.7 = (f32[128,512]{1,0:T(8,128)}, f32[128,512]{1,0:T(8,128)S(1)}, u32[]{:S(2)}) copy-start(f32[128,512]{1,0:T(8,128)S(1)} %sub.18) | copy-start | bytes 786436
  328.7 22.4 %copy-start.8 = (bf16[128,512]{1,0:T(8,128)(2,1)}, bf16[128,512]{1,0:T(8,128)(2,1)S(1)}, u32[]{:S(2)}) copy-start(bf16[128,512]{1,0:T(8,128)(2,1)S(1)} %fusion.6) | copy-start | bytes 393220
Sparse Core Ops, SparseCore 0:
  44.9 100.8 all-gather.3
  184.2 36.0 reduce-scatter.1
  223.7 19.6 all-gather.5
  250.6 75.6 all-reduce.2
  327.7 18.7 all-gather.7
where the time goes:
time: 360 us; the launch traced here: 359 us
  waiting for transfers between devices  227 us (63%)
  local copies, waits for them, and re-layouts  37.5 us (10%)
  matrix products  27.1 us (8%)
  other arithmetic  26.2 us (7%)
  starting transfers between devices  19.3 us (5%)
  between operations  14.4 us (4%)
  blocking collectives  7.15 us (2%)
    all_gather x1, waiting for transfers between devices, on_device(): held = lax.all_gather(mine, 'row', axis=2, tiled=True)  95.2 us
    psum x1, waiting for transfers between devices, on_device(): lax.psum((contract_rows(by_slot(col_a, own_a, live_a), factor_a), contrac...  69.1 us
    reduce_scatter x1, waiting for transfers between devices, on_device(): lax.psum_scatter(part, 'col', scatter_dimension=2, tiled=True)  34.1 us
    ppermute x7, starting transfers between devices, on_device(): piece = lax.ppermute(piece, ('row', 'col'), pairs)  18.9 us
    dot_general x2, matrix products, partial_product(): jnp.dot(trailing, spread, preferred_element_type=jnp.float32)  17 us
    all_gather x1, waiting for transfers between devices, on_device(): whole_a = lax.all_gather(col_a, 'col', axis=1, tiled=True)  13.2 us
    gather x2, local copies, waits for them, and re-layouts, partial_product(): jnp.take(held[node].reshape(fanout * slots, block, width), source, axis=0)  8.76 us
    all_gather x1, waiting for transfers between devices, on_device(): lax.all_gather(col_b, 'col', axis=1, tiled=True)  8.72 us
  transfers between devices with their start and end apart: 12, of which 7 were waited for; matrix products, arithmetic and copies ran while one was open for 9% of the time, Pallas kernels for 0%

commit v1 on v0

--- a/solution.py
+++ b/solution.py
@@ -59,7 +59,14 @@
         ],
         axis=1,
     )
-    held = lax.all_gather(mine, "row", axis=2, tiled=True)
+    size = lax.axis_size("row")
+    right = [(i, (i + 1) % size) for i in range(size)]
+    terms = [mine]
+    for far in range(1, size):
+        terms = [lax.ppermute(terms[0], "row", right), *terms]
+    out = jnp.concatenate(terms, axis=2)
+    offset = (lax.axis_index("row") + 1) * terms[-1].shape[2]
+    held = jnp.roll(out, offset, axis=2)
     owners = col_index + jnp.arange(fanout, dtype=jnp.int32) * col_count
 
     def partial_product(node, rows, counts):

time: 360 us -> 410 us (1.14)
  waiting for transfers between devices: 227 us -> 260 us
  local copies, waits for them, and re-layouts: 37.5 us -> 49.8 us
  starting transfers between devices: 19.3 us -> 24.5 us
    ppermute x0 -> x7, waiting for transfers between devices: none -> 116 us  [on_device(): terms = [lax.ppermute(terms[0], 'row', right), *terms]]
    all_gather x1 -> x0, waiting for transfers between devices: 95.2 us -> none  [on_device(): held = lax.all_gather(mine, 'row', axis=2, tiled=True)]
    unnamed x34 -> x56, local copies, waits for them, and re-layouts: 6.36 us -> 20.3 us
    reduce_scatter x1, waiting for transfers between devices: 34.1 us -> 46.6 us  [on_device(): lax.psum_scatter(part, 'col', scatter_dimension=2, tiled=True)]
    ppermute x0 -> x7, starting transfers between devices: none -> 5.17 us  [on_device(): terms = [lax.ppermute(terms[0], 'row', right), *terms]]
  transfers between devices with their start and end apart: 12 -> 18, of which waited for: 7 -> 13; matrix products, arithmetic and copies ran while one was open for 9% -> 8% of each run, Pallas kernels for 0% -> 0%
where the time goes in v1:
time: 410 us; the launch traced here: 409 us
  waiting for transfers between devices  260 us (63%)
  local copies, waits for them, and re-layouts  49.8 us (12%)
  matrix products  27.1 us (7%)
  other arithmetic  25.5 us (6%)
  starting transfers between devices  24.5 us (6%)
  between operations  14.5 us (4%)
  blocking collectives  7.15 us (2%)
    ppermute x7, waiting for transfers between devices, on_device(): terms = [lax.ppermute(terms[0], 'row', right), *terms]  116 us
    psum x1, waiting for transfers between devices, on_device(): lax.psum((contract_rows(by_slot(col_a, own_a, live_a), factor_a), contrac...  69.1 us
    reduce_scatter x1, waiting for transfers between devices, on_device(): lax.psum_scatter(part, 'col', scatter_dimension=2, tiled=True)  46.6 us
    unnamed x56, local copies, waits for them, and re-layouts  20.3 us
    ppermute x7, starting transfers between devices, on_device(): piece = lax.ppermute(piece, ('row', 'col'), pairs)  18.9 us
    dot_general x2, matrix products, partial_product(): jnp.dot(trailing, spread, preferred_element_type=jnp.float32)  17 us
    all_gather x1, waiting for transfers between devices, on_device(): whole_a = lax.all_gather(col_a, 'col', axis=1, tiled=True)  13.1 us
    gather x2, local copies, waits for them, and re-layouts, partial_product(): jnp.take(held[node].reshape(fanout * slots, block, width), source, axis=0)  8.87 us
  transfers between devices with their start and end apart: 18, of which 13 were waited for; matrix products, arithmetic and copies ran while one was open for 8% of the time, Pallas kernels for 0%

profile of v1, /device:TPU:0, one launch (start us, length us, event | category | flops | bytes accessed | tf_op | source)
XLA Modules:
  0.0 408.9 jit_solution(918490085836492734)
XLA Ops:
  7.3 2.9 fusion.22
  10.2 5.6 %collective-permute-start = (bf16[2,192,512]{2,1,0:T(8,128)(2,1)}, bf16[2,192,512]{2,1,0:T(8,128)(2,1)}, u32[]{:S(2)}, u32[]{:S(2)}) collective-permute-start(bf16[2,192,512]{2,1,0:T(8,128)(2,1)} %get-tuple-element.26), channel_id=1, source_target_pairs={{0,4},{5,9},{10,14},{15,19},{16,20},{21,25},{26,30},{31,3}} | collective-permute-start | bytes 1179656 | tf_op jit(solution)/shard_map/ppermute | solution.py:50
  17.9 2.0 collective-permute-start.2
  20.0 4.5 %collective-permute-start.3 = (bf16[2,192,512]{2,1,0:T(8,128)(2,1)S(1)}, bf16[2,192,512]{2,1,0:T(8,128)(2,1)}, u32[]{:S(2)}, u32[]{:S(2)}) collective-permute-start(bf16[2,192,512]{2,1,0:T(8,128)(2,1)S(1)} %get-tuple-element.29), channel_id=1, source_target_pairs={{0,16},{5,21},{10,26},{15,31},{16,0},{21,5},{26,10},{31,15}} | collective-permute-start | bytes 1179656 | tf_op jit(solution)/shard_map/ppermute | solution.py:50
  24.5 2.1 collective-permute-start.4
  37.3 2.3 collective-permute-done.5
  39.5 4.2 %collective-permute-done.6 = bf16[2,192,512]{2,1,0:T(8,128)(2,1)S(1)} collective-permute-done((bf16[2,192,512]{2,1,0:T(8,128)(2,1)S(1)}, bf16[2,192,512]{2,1,0:T(8,128)(2,1)S(1)}, u32[]{:S(2)}, u32[]{:S(2)}) %collective-permute-start.6) | collective-permute-done | bytes 393248 | tf_op jit(solution)/shard_map/ppermute | solution.py:50
  44.0 19.9 %collective-permute-done.7 = bf16[2,2,192,512]{3,2,0,1:T(8,128)(2,1)S(1)} collective-permute-done((bf16[2,2,192,512]{3,2,0,1:T(8,128)(2,1)S(1)}, bf16[2,2,192,512]{3,2,0,1:T(8,128)(2,1)S(1)}, u32[]{:S(2)}, u32[]{:S(2)}) %collective-permute-start.7) | collective-permute-done | bytes 786464 | tf_op jit(solution)/shard_map/ppermute | solution.py:66
  64.8 18.6 %collective-permute-done.8 = bf16[2,2,192,512]{3,2,0,1:T(8,128)(2,1)S(1)} collective-permute-done((bf16[2,2,192,512]{3,2,0,1:T(8,128)(2,1)S(1)}, bf16[2,2,192,512]{3,2,0,1:T(8,128)(2,1)S(1)}, u32[]{:S(2)}, u32[]{:S(2)}) %collective-permute-start.8) | collective-permute-done | bytes 786464 | tf_op jit(solution)/shard_map/ppermute | solution.py:66
  84.3 17.9 %collective-permute-done.9 = bf16[2,2,192,512]{3,2,0,1:T(8,128)(2,1)} collective-permute-done((bf16[2,2,192,512]{3,2,0,1:T(8,128)(2,1)S(1)}, bf16[2,2,192,512]{3,2,0,1:T(8,128)(2,1)}, u32[]{:S(2)}, u32[]{:S(2)}) %collective-permute-start.9) | collective-permute-done | bytes 786464 | tf_op jit(solution)/shard_map/ppermute | solution.py:66
  102.8 16.8 %collective-permute-done.10 = bf16[2,2,192,512]{3,2,0,1:T(8,128)(2,1)} collective-permute-done((bf16[2,2,192,512]{3,2,0,1:T(8,128)(2,1)}, bf16[2,2,192,512]{3,2,0,1:T(8,128)(2,1)}, u32[]{:S(2)}, u32[]{:S(2)}) %collective-permute-start.10) | collective-permute-done | bytes 786464 | tf_op jit(solution)/shard_map/ppermute | solution.py:66
  122.4 13.8 %collective-permute-done.11 = bf16[2,2,192,512]{3,2,0,1:T(8,128)(2,1)} collective-permute-done((bf16[2,2,192,512]{3,2,0,1:T(8,128)(2,1)}, bf16[2,2,192,512]{3,2,0,1:T(8,128)(2,1)}, u32[]{:S(2)}, u32[]{:S(2)}) %collective-permute-start.11) | collective-permute-done | bytes 786464 | tf_op jit(solution)/shard_map/ppermute | solution.py:66
  136.2 2.6 collective-permute-start.12
  141.1 13.7 %collective-permute-done.12 = bf16[2,2,192,512]{3,2,0,1:T(8,128)(2,1)} collective-permute-done((bf16[2,2,192,512]{3,2,0,1:T(8,128)(2,1)}, bf16[2,2,192,512]{3,2,0,1:T(8,128)(2,1)}, u32[]{:S(2)}, u32[]{:S(2)}) %collective-permute-start.12) | collective-permute-done | bytes 786464 | tf_op jit(solution)/shard_map/ppermute | solution.py:66
  157.2 15.3 %collective-permute-done.13 = bf16[2,2,192,512]{3,2,0,1:T(8,128)(2,1)} collective-permute-done((bf16[2,2,192,512]{3,2,0,1:T(8,128)(2,1)}, bf16[2,2,192,512]{3,2,0,1:T(8,128)(2,1)}, u32[]{:S(2)}, u32[]{:S(2)}) %collective-permute-start.13) | collective-permute-done | bytes 786464 | tf_op jit(solution)/shard_map/ppermute | solution.py:66
  185.0 4.0 constant_dynamic-slice_fusion.2
  189.0 4.4 %gather_fusion.2 = bf16[24,128,512]{2,1,0:T(8,128)(2,1)} fusion(bf16[24,128,512]{2,1,0:T(8,128)(2,1)} %bitcast.98, s32[1024]{0:T(1024)S(1)} %pad_clamp_fusion.3), kind=kCustom, calls=%fused_computation.2.clone | custom fusion | bytes 6291552 | tf_op jit(solution)/shard_map/jit(_take)/gather | solution.py:79
  193.5 2.3 select_select_fusion.1
  195.8 9.0 %fusion = bf16[1,1536,512]{1,2,0:T(8,128)(2,1)} fusion(bf16[3072,512]{1,0:T(8,128)(2,1)S(1)} %bitcast.101, bf16[1536,3072]{1,0:T(8,128)(2,1)} %param.20), kind=kOutput, calls=%fused_computation.32 | convolution fusion | flops 4832624640 | bytes 14155776 | tf_op jit(solution)/shard_map/dot_general | solution.py:81
  204.8 4.4 %gather_fusion.5 = bf16[24,128,512]{2,1,0:T(8,128)(2,1)} fusion(bf16[24,128,512]{2,1,0:T(8,128)(2,1)} %bitcast.97, s32[1024]{0:T(1024)S(1)} %pad_clamp_fusion.2), kind=kCustom, calls=%fused_computation.7.clone | custom fusion | bytes 6291552 | tf_op jit(solution)/shard_map/jit(_take)/gather | solution.py:79
  209.2 2.3 select_select_fusion
  211.5 8.0 %fusion.1 = bf16[1,1536,512]{1,2,0:T(8,128)(2,1)S(1)} fusion(bf16[3072,512]{1,0:T(8,128)(2,1)S(1)} %bitcast.102, bf16[1536,3072]{1,0:T(8,128)(2,1)} %param.20), kind=kOutput, calls=%fused_computation.33 | convolution fusion | flops 4832624640 | bytes 14155776 | tf_op jit(solution)/shard_map/dot_general | solution.py:81
  223.6 46.6 %reduce-scatter.2.cloned.1.call-done = bf16[2,1536,128]{1,2,0:T(8,128)(2,1)} async-done(((bf16[2,1536,512]{1,2,0:T(8,128)(2,1)}), bf16[2,1536,128]{1,2,0:T(8,128)(2,1)}) %reduce-scatter.2.cloned.1.call-update) | async-done | bytes 786448 | tf_op jit(solution)/shard_map/reduce_scatter | solution.py:84
  277.6 2.5 fusion.37
  280.1 13.1 %all-gather.3.cloned.1.call-done = bf16[1536,512]{0,1:T(8,128)(2,1)} async-done(((bf16[1536,128]{0,1:T(8,128)(2,1)}), bf16[1536,512]{0,1:T(8,128)(2,1)}) %all-gather.3.cloned.1.call-update) | async-done | bytes 1572880 | tf_op jit(solution)/shard_map/all_gather | solution.py:96
  300.9 2.6 copy.27
  303.5 2.1 gather_fusion.6
  307.0 69.1 %all-reduce.3.cloned.1.call-done = (f32[128,512]{1,0:T(8,128)}, f32[128,512]{1,0:T(8,128)}, f32[128,512]{1,0:T(8,128)}) async-done(((f32[128,512]{1,0:T(8,128)}, f32[128,512]{1,0:T(8,128)}, f32[128,512]{1,0:T(8,128)}), (f32[128,512]{1,0:T(8,128)}, f32[128,512]{1,0:T(8,128)}, f32[128,512]{1,0:T(8,128)})) %all-reduce.3.cloned.1.call-update) | async-done | bytes 786448 | tf_op jit(solution)/shard_map/psum | solution.py:102
  378.5 7.1 %all_gather.11 = bf16[512,512]{1,0:T(8,128)(2,1)S(1)} all-gather(bf16[128,512]{1,0:T(8,128)(2,1)S(1)} %fusion.6), channel_id=1, replica_groups=mesh['row'=8,'col'=4] {'col'}, dimensions={0}, use_global_device_ids=true | all-gather | bytes 655360 | tf_op jit(solution)/shard_map/all_gather | solution.py:117
  387.6 8.7 %all-gather.5.cloned.1.call-done = bf16[1536,512]{0,1:T(8,128)(2,1)} async-done(((bf16[1536,128]{0,1:T(8,128)(2,1)}), bf16[1536,512]{0,1:T(8,128)(2,1)}) %all-gather.5.cloned.1.call-update) | async-done | bytes 1572880 | tf_op jit(solution)/shard_map/all_gather | solution.py:101
  396.3 2.6 copy.30
  398.9 2.1 gather_fusion.8
  (143 shorter events, 61.3 us)
Async XLA Ops:
  7.2 286.1 %copy-start = (bf16[512,512]{1,0:T(8,128)(2,1)S(1)}, bf16[512,512]{1,0:T(8,128)(2,1)}, u32[]{:S(2)}) copy-start(bf16[512,512]{1,0:T(8,128)(2,1)} %param.27) | copy-start | bytes 1572868
  7.2 19.4 %copy-start.3 = (bf16[1536,512]{1,0:T(8,128)(2,1)S(1)}, bf16[1536,512]{1,0:T(8,128)(2,1)}, u32[]{:S(2)}) copy-start(bf16[1536,512]{1,0:T(8,128)(2,1)} %param.26) | copy-start | bytes 4718596
  7.2 263.0 %reduce-scatter.2.cloned.1.call-start = ((), (), s32[]{:S(2)}) async-start(), calls=%async_computation.1 | async-start | bytes 3932160 | tf_op jit(solution)/shard_map/reduce_scatter | solution.py:84
  10.2 19.1 %collective-permute-start = (bf16[2,192,512]{2,1,0:T(8,128)(2,1)}, bf16[2,192,512]{2,1,0:T(8,128)(2,1)}, u32[]{:S(2)}, u32[]{:S(2)}) collective-permute-start(bf16[2,192,512]{2,1,0:T(8,128)(2,1)} %get-tuple-element.26), channel_id=1, source_target_pairs={{0,4},{5,9},{10,14},{15,19},{16,20},{21,25},{26,30},{31,3}} | collective-permute-start | bytes 1179656 | tf_op jit(solution)/shard_map/ppermute | solution.py:50
  15.9 15.8 %collective-permute-start.1 = (bf16[2,192,512]{2,1,0:T(8,128)(2,1)}, bf16[2,192,512]{2,1,0:T(8,128)(2,1)}, u32[]{:S(2)}, u32[]{:S(2)}) collective-permute-start(bf16[2,192,512]{2,1,0:T(8,128)(2,1)} %get-tuple-element.27), channel_id=1, source_target_pairs={{0,8},{5,13},{10,18},{15,23},{16,24},{21,29},{26,2},{31,7}} | collective-permute-start | bytes 1179656 | tf_op jit(solution)/shard_map/ppermute | solution.py:50
  17.9 16.2 %collective-permute-start.2 = (bf16[2,192,512]{2,1,0:T(8,128)(2,1)}, bf16[2,192,512]{2,1,0:T(8,128)(2,1)}, u32[]{:S(2)}, u32[]{:S(2)}) collective-permute-start(bf16[2,192,512]{2,1,0:T(8,128)(2,1)} %get-tuple-element.28), channel_id=1, source_target_pairs={{0,12},{5,17},{10,22},{15,27},{16,28},{21,1},{26,6},{31,11}} | collective-permute-start | bytes 1179656 | tf_op jit(solution)/shard_map/ppermute | solution.py:50
  20.0 15.2 %collective-permute-start.3 = (bf16[2,192,512]{2,1,0:T(8,128)(2,1)S(1)}, bf16[2,192,512]{2,1,0:T(8,128)(2,1)}, u32[]{:S(2)}, u32[]{:S(2)}) collective-permute-start(bf16[2,192,512]{2,1,0:T(8,128)(2,1)S(1)} %get-tuple-element.29), channel_id=1, source_target_pairs={{0,16},{5,21},{10,26},{15,31},{16,0},{21,5},{26,10},{31,15}} | collective-permute-start | bytes 1179656 | tf_op jit(solution)/shard_map/ppermute | solution.py:50
  24.5 11.7 %collective-permute-start.4 = (bf16[2,192,512]{2,1,0:T(8,128)(2,1)S(1)}, bf16[2,192,512]{2,1,0:T(8,128)(2,1)}, u32[]{:S(2)}, u32[]{:S(2)}) collective-permute-start(bf16[2,192,512]{2,1,0:T(8,128)(2,1)S(1)} %get-tuple-element.30), channel_id=1, source_target_pairs={{0,20},{5,25},{10,30},{15,3},{16,4},{21,9},{26,14},{31,19}} | collective-permute-start | bytes 1179656 | tf_op jit(solution)/shard_map/ppermute | solution.py:50
  29.4 10.1 %collective-permute-start.5 = (bf16[2,192,512]{2,1,0:T(8,128)(2,1)S(1)}, bf16[2,192,512]{2,1,0:T(8,128)(2,1)S(1)}, u32[]{:S(2)}, u32[]{:S(2)}) collective-permute-start(bf16[2,192,512]{2,1,0:T(8,128)(2,1)S(1)} %fusion.16), channel_id=1, source_target_pairs={{0,24},{5,29},{10,2},{15,7},{16,8},{21,13},{26,18},{31,23}} | collective-permute-start | bytes 1179656 | tf_op jit(solution)/shard_map/ppermute | solution.py:50
  31.7 12.0 %collective-permute-start.6 = (bf16[2,192,512]{2,1,0:T(8,128)(2,1)S(1)}, bf16[2,192,512]{2,1,0:T(8,128)(2,1)S(1)}, u32[]{:S(2)}, u32[]{:S(2)}) collective-permute-start(bf16[2,192,512]{2,1,0:T(8,128)(2,1)S(1)} %get-tuple-element.25), channel_id=1, source_target_pairs={{0,28},{5,1},{10,6},{15,11},{16,12},{21,17},{26,22},{31,27}} | collective-permute-start | bytes 1179656 | tf_op jit(solution)/shard_map/ppermute | solution.py:50
  35.1 67.0 %copy-start.1 = (s32[8]{0:T(128)S(1)}, s32[8]{0:T(128)}, u32[]{:S(2)}) copy-start(s32[8]{0:T(128)} %param.22) | copy-start | bytes 100
  36.2 84.3 %copy-start.16 = (s32[8,12]{1,0:T(8,128)S(1)}, s32[8,12]{1,0:T(8,128)}, u32[]{:S(2)}) copy-start(s32[8,12]{1,0:T(8,128)} %param.21) | copy-start | bytes 1156
  36.2 84.8 %copy-start.17 = (s32[8,12]{1,0:T(8,128)S(1)}, s32[8,12]{1,0:T(8,128)}, u32[]{:S(2)}) copy-start(s32[8,12]{1,0:T(8,128)} %param.24) | copy-start | bytes 1156
  36.2 85.4 %copy-start.2 = (s32[8]{0:T(128)S(1)}, s32[8]{0:T(128)}, u32[]{:S(2)}) copy-start(s32[8]{0:T(128)} %param.25) | copy-start | bytes 100
  43.9 20.0 %collective-permute-start.7 = (bf16[2,2,192,512]{3,2,0,1:T(8,128)(2,1)S(1)}, bf16[2,2,192,512]{3,2,0,1:T(8,128)(2,1)S(1)}, u32[]{:S(2)}, u32[]{:S(2)}) collective-permute-start(bf16[2,2,192,512]{3,2,0,1:T(8,128)(2,1)S(1)} %pad_maximum_fusion.1), channel_id=1, source_target_pairs={{0,4},{4,8},{8,12},{12,16},{16,20},{20,24},{24,28},{28,0},{1,5},{5... | collective-permute-start | bytes 2359304 | tf_op jit(solution)/shard_map/ppermute | solution.py:66
  64.8 18.6 %collective-permute-start.8 = (bf16[2,2,192,512]{3,2,0,1:T(8,128)(2,1)S(1)}, bf16[2,2,192,512]{3,2,0,1:T(8,128)(2,1)S(1)}, u32[]{:S(2)}, u32[]{:S(2)}) collective-permute-start(bf16[2,2,192,512]{3,2,0,1:T(8,128)(2,1)S(1)} %collective-permute-done.7), channel_id=1, source_target_pairs={{0,4},{4,8},{8,12},{12,16},{16,20},{20,24},{24,28},{28,0},{1,5},{5... | collective-permute-start | bytes 2359304 | tf_op jit(solution)/shard_map/ppermute | solution.py:66
  84.3 17.9 %collective-permute-start.9 = (bf16[2,2,192,512]{3,2,0,1:T(8,128)(2,1)S(1)}, bf16[2,2,192,512]{3,2,0,1:T(8,128)(2,1)}, u32[]{:S(2)}, u32[]{:S(2)}) collective-permute-start(bf16[2,2,192,512]{3,2,0,1:T(8,128)(2,1)S(1)} %collective-permute-done.8), channel_id=1, source_target_pairs={{0,4},{4,8},{8,12},{12,16},{16,20},{20,24},{24,28},{28,0},{1,5},{5... | collective-permute-start | bytes 2359304 | tf_op jit(solution)/shard_map/ppermute | solution.py:66
  102.1 17.4 %collective-permute-start.10 = (bf16[2,2,192,512]{3,2,0,1:T(8,128)(2,1)}, bf16[2,2,192,512]{3,2,0,1:T(8,128)(2,1)}, u32[]{:S(2)}, u32[]{:S(2)}) collective-permute-start(bf16[2,2,192,512]{3,2,0,1:T(8,128)(2,1)} %collective-permute-done.9), channel_id=1, source_target_pairs={{0,4},{4,8},{8,12},{12,16},{16,20},{20,24},{24,28},{28,0},{1,5},{5... | collective-permute-start | bytes 2359304 | tf_op jit(solution)/shard_map/ppermute | solution.py:66
  119.6 16.6 %collective-permute-start.11 = (bf16[2,2,192,512]{3,2,0,1:T(8,128)(2,1)}, bf16[2,2,192,512]{3,2,0,1:T(8,128)(2,1)}, u32[]{:S(2)}, u32[]{:S(2)}) collective-permute-start(bf16[2,2,192,512]{3,2,0,1:T(8,128)(2,1)} %collective-permute-done.10), channel_id=1, source_target_pairs={{0,4},{4,8},{8,12},{12,16},{16,20},{20,24},{24,28},{28,0},{1,5},{5... | collective-permute-start | bytes 2359304 | tf_op jit(solution)/shard_map/ppermute | solution.py:66
  136.2 18.6 %collective-permute-start.12 = (bf16[2,2,192,512]{3,2,0,1:T(8,128)(2,1)}, bf16[2,2,192,512]{3,2,0,1:T(8,128)(2,1)}, u32[]{:S(2)}, u32[]{:S(2)}) collective-permute-start(bf16[2,2,192,512]{3,2,0,1:T(8,128)(2,1)} %collective-permute-done.11), channel_id=1, source_target_pairs={{0,4},{4,8},{8,12},{12,16},{16,20},{20,24},{24,28},{28,0},{1,5},{5... | collective-permute-start | bytes 2359304 | tf_op jit(solution)/shard_map/ppermute | solution.py:66
  154.8 17.7 %collective-permute-start.13 = (bf16[2,2,192,512]{3,2,0,1:T(8,128)(2,1)}, bf16[2,2,192,512]{3,2,0,1:T(8,128)(2,1)}, u32[]{:S(2)}, u32[]{:S(2)}) collective-permute-start(bf16[2,2,192,512]{3,2,0,1:T(8,128)(2,1)} %collective-permute-done.12), channel_id=1, source_target_pairs={{0,4},{4,8},{8,12},{12,16},{16,20},{20,24},{24,28},{28,0},{1,5},{5... | collective-permute-start | bytes 2359304 | tf_op jit(solution)/shard_map/ppermute | solution.py:66
  173.7 4.9 %copy-start.9 = (bf16[2,2,192,512]{3,2,0,1:T(8,128)(2,1)S(1)}, bf16[2,2,192,512]{3,2,0,1:T(8,128)(2,1)}, u32[]{:S(2)}) copy-start(bf16[2,2,192,512]{3,2,0,1:T(8,128)(2,1)} %copy-done.8) | copy-start | bytes 2359300
  175.0 3.7 copy-start.7
  211.5 8.0 %copy-start.10 = (bf16[1,1536,512]{1,2,0:T(8,128)(2,1)S(1)}, bf16[1,1536,512]{1,2,0:T(8,128)(2,1)}, u32[]{:S(2)}) copy-start(bf16[1,1536,512]{1,2,0:T(8,128)(2,1)} %fusion) | copy-start | bytes 4718596
  221.5 71.8 %all-gather.3.cloned.1.call-start = ((), (), s32[]{:S(2)}) async-start(), calls=%async_computation.2 | async-start | bytes 1966080 | tf_op jit(solution)/shard_map/all_gather | solution.py:96
  273.4 102.7 %all-reduce.3.cloned.1.call-start = ((), (), s32[]{:S(2)}) async-start(), calls=%async_computation.4 | async-start | bytes 1572864 | tf_op jit(solution)/shard_map/psum | solution.py:102
  295.3 5.0 %copy-start.5 = (bf16[1536,128]{0,1:T(8,128)(2,1)}, bf16[1536,128]{0,1:T(8,128)(2,1)S(1)}, u32[]{:S(2)}) copy-start(bf16[1536,128]{0,1:T(8,128)(2,1)S(1)} %fusion.4) | copy-start | bytes 1179652
  300.3 96.0 %all-gather.5.cloned.1.call-start = ((), (), s32[]{:S(2)}) async-start(), calls=%async_computation.3 | async-start | bytes 1966080 | tf_op jit(solution)/shard_map/all_gather | solution.py:101
  303.5 72.6 %copy-start.14 = (f32[128,512]{1,0:T(8,128)S(1)}, f32[128,512]{1,0:T(8,128)}, u32[]{:S(2)}) copy-start(f32[128,512]{1,0:T(8,128)} %param.28) | copy-start | bytes 786436
  305.6 80.1 %copy-start.15 = (f32[128,512]{1,0:T(8,128)S(1)}, f32[128,512]{1,0:T(8,128)}, u32[]{:S(2)}) copy-start(f32[128,512]{1,0:T(8,128)} %param.29) | copy-start | bytes 786436
  377.1 21.8 %copy-start.11 = (f32[128,512]{1,0:T(8,128)}, f32[128,512]{1,0:T(8,128)S(1)}, u32[]{:S(2)}) copy-start(f32[128,512]{1,0:T(8,128)S(1)} %sub.23) | copy-start | bytes 786436
  378.5 22.5 %copy-start.12 = (bf16[128,512]{1,0:T(8,128)(2,1)}, bf16[128,512]{1,0:T(8,128)(2,1)S(1)}, u32[]{:S(2)}) copy-start(bf16[128,512]{1,0:T(8,128)(2,1)S(1)} %fusion.6) | copy-start | bytes 393220
  (4 other events, 5.4 us)
Sparse Core Ops, SparseCore 0:
  221.6 48.5 reduce-scatter.1
  273.6 19.6 all-gather.2
  300.4 75.6 all-reduce.2
  377.5 18.7 all-gather.4
